TPU v7x, 256 devices: a whole 4x4x8 slice. The times are simulated.
256 devices in a mesh: rows: 32 (over x, z_lo, core), cols: 8 (over y, z_hi).
Axes of the slice: x: 4, y: 4, z: 8 (z_hi: 2, z_lo: 4; z = z_hi * 4 + z_lo), core: 2. Of those that a mesh axis runs over, the one named last changes fastest.
Arguments:
- matrix_blocks: bfloat16 [8192, 64, 1728], P(('rows', 'cols')), may hold values from -0.75 to 0.75
- restrict: bfloat16 [8192, 4096], P(('rows', 'cols')), may hold values from -1.5 to 1.5
- columns: int32 [8192, 27], P(('rows', 'cols')), may hold values from 0 to 767
- counts: int32 [8192], P(('rows', 'cols')), may hold values from 8 to 27, as said below
- aggregate: int32 [8192], P(('rows', 'cols')), may hold values from 0 to 1
Outputs:
- coarse: float32 [512, 64, 3072], P(('rows', 'cols'))
Inputs may be any that keep to these rules, and one draw needn't show every extreme that they name: `counts`: used slots are the first ones of a row; some row uses all 27.
All inputs are finite; a program needn't handle non-finite values.
Results may differ from a plain program's by a relative error of at most 0.0029.
Values may be sent and summed in bfloat16 or wider, within the bound.
A program may use at most 192 MiB of HBM per device.

v0:
```python
import functools

import jax
import jax.numpy as jnp
from jax import lax
from jax.experimental import pallas as pl
from jax.experimental.pallas import tpu as pltpu
from jax.sharding import PartitionSpec as P

BLK = 64
SLOTS = 27
ROWS_DEV = 32
AGG_DEV = 2
Y = 4
NZ = 4
TILES = ROWS_DEV // 2
PIECE = TILES * 4 + 1
PAIRS = (SLOTS + 1) // 2
MESH = pl.DeviceIdType.MESH
ORDER = {
    "own_b": 4, "own_f": 5, "near_0": 8, "other_0": 10, "own_2": 12, "other_f": 17, "near_b": 17.5, "other_b": 18,
    "other_2": 22, "back_0": 24, "back_f": 27, "near_f": 27.5, "back_b": 28, "near_2": 28.5, "back_2": 31,
}


def gather_kernel(n_rows, with_left, chunks, pace, x_ref, a_hbm, g_ref, l_hbm, a_buf, l_buf, send_sem, recv_sem, own_sem, a_sem, l_sem):
    r = lax.axis_index("rows")
    col = lax.axis_index("cols")
    y = col // 2
    zh = lax.rem(col, 2)
    c = lax.rem(r, 2)
    zlo = lax.rem(r // 2, NZ)
    d = 1 - 2 * c
    partner = r + d
    far = r - d
    has_far = jnp.logical_and(far >= 0, far < n_rows)
    turn = jnp.logical_or(
        jnp.logical_and(zlo == 0, c == 0), jnp.logical_and(zlo == NZ - 1, c == 1)
    ).astype(jnp.int32)
    near_z = lax.rem(zh + turn, 2)
    other_z = 1 - near_z
    t3 = jnp.where(has_far, far, r)
    z3 = jnp.where(has_far, other_z, 1 - zh)
    r3_row = jnp.where(has_far, far, partner)
    r3_z = jnp.where(has_far, near_z, zh)

    def ring(step):
        return lax.rem(y + step + 2 * Y, Y)

    yf, yb, y2 = ring(d), ring(-d), ring(2)

    def dev(row, yy, zz):
        return (row, yy * 2 + zz)

    me_near = dev(far, y, near_z)
    me_other = dev(t3, y, z3)
    me_part = dev(partner, y, zh)
    me_yf = dev(r, yf, zh)
    me_yb = dev(r, yb, zh)
    me_r3 = dev(r3_row, y, r3_z)

    def slot(row, slab, yy, zz):
        return (slab - row + 1) * (2 * Y) + yy * 2 + zz

    size = x_ref.shape[0]
    cuts = [size // chunks * k for k in range(chunks)] + [size]

    def copy(src, slab, yy, zz, to, index, part):
        span = pl.ds(cuts[part], cuts[part + 1] - cuts[part])
        to_slot = slot(to[0], slab, yy, zz)
        return pltpu.make_async_remote_copy(
            src_ref=src.at[span],
            dst_ref=g_ref.at[to_slot, span],
            send_sem=send_sem.at[index, part],
            recv_sem=recv_sem.at[to_slot, part],
            device_id=to,
            device_id_type=MESH,
        )

    def own_copy(to, index, part):
        return copy(x_ref, r, y, zh, to, index, part)

    def relay(slab, yy, zz, to, index, part):
        return copy(g_ref.at[slot(r, slab, yy, zz)], slab, yy, zz, to, index, part)

    def arrived(slab, yy, zz, part):
        span = pl.ds(cuts[part], cuts[part + 1] - cuts[part])
        s = slot(r, slab, yy, zz)
        pltpu.make_async_remote_copy(
            src_ref=g_ref.at[s, span],
            dst_ref=g_ref.at[s, span],
            send_sem=send_sem.at[0, part],
            recv_sem=recv_sem.at[s, part],
            device_id=me_part,
            device_id_type=MESH,
        ).wait_recv()

    own_piece, far_near, far_other, own_other = (r, zh), (far, near_z), (t3, z3), (r, 1 - zh)
    stages = {
        "own_b": (own_piece, yb, False, [(me_yf, 10), (me_part, 11)]),
        "own_f": (own_piece, yf, False, [(me_part, 12)]),
        "own_2": (own_piece, y2, False, [(me_part, 17)]),
        "near_0": (far_near, y, True, [(me_yf, 8), (me_yb, 9)]),
        "near_b": (far_near, yb, True, [(me_yf, 16)]),
        "near_f": (far_near, yf, True, []),
        "near_2": (far_near, y2, True, []),
        "other_0": (far_other, y, False, [(me_yf, 5), (me_yb, 6), (me_r3, 7)]),
        "other_f": (far_other, yf, False, [(me_yb, 13), (me_r3, 15)]),
        "other_b": (far_other, yb, False, [(me_r3, 14)]),
        "other_2": (far_other, y2, False, [(me_r3, 18)]),
        "back_0": (own_other, y, True, [(me_part, 19)]),
        "back_f": (own_other, yf, True, [(me_part, 20)]),
        "back_b": (own_other, yb, True, [(me_part, 21)]),
        "back_2": (own_other, y2, True, [(me_part, 22)]),
    }

    def step(name, part):
        (slab, zz), yy, needs_far, targets = stages[name]

        def run():
            arrived(slab, yy, zz, part)
            for to, index in targets:
                relay(slab, yy, zz, to, index, part).start()

        if needs_far:
            pl.when(has_far)(run)
        else:
            run()

    def sent(name, part):
        (slab, zz), yy, needs_far, targets = stages[name]

        def run():
            for to, index in targets:
                relay(slab, yy, zz, to, index, part).wait_send()

        if needs_far:
            pl.when(has_far)(run)
        else:
            run()

    groups = ROWS_DEV // 4

    def a_copy(k):
        rows = pl.ds(k * 4, 4)
        return pltpu.make_async_copy(a_hbm.at[rows], a_buf.at[rows], a_sem.at[k])

    def l_copy(k):
        rows = pl.ds(k * 4, 4)
        return pltpu.make_async_copy(l_buf.at[rows], l_hbm.at[rows], l_sem.at[k])

    if with_left:

        @pl.loop(0, groups)
        def _(k):
            a_copy(k).start()

    barrier = pltpu.get_barrier_semaphore()
    for to in (me_other, me_part, me_yf, me_yb):
        pl.semaphore_signal(barrier, inc=1, device_id=to, device_id_type=MESH)

    @pl.when(has_far)
    def _():
        pl.semaphore_signal(barrier, inc=1, device_id=me_near, device_id_type=MESH)

    pl.semaphore_wait(barrier, 4 + has_far.astype(jnp.int32))

    for part in range(chunks):
        @pl.when(has_far)
        def _(part=part):
            own_copy(me_near, 1, part).start()

        own_copy(me_other, 0, part).start()
        own_copy(me_yf, 2, part).start()
        own_copy(me_yb, 3, part).start()
        own_copy(me_part, 4, part).start()

    mine = pltpu.make_async_copy(x_ref, g_ref.at[slot(r, r, y, zh)], own_sem)
    mine.start()

    if with_left:
        low = lax.broadcasted_iota(jnp.int32, (BLK, 128), 1) < BLK
        zero = jnp.zeros((BLK, 128), jnp.bfloat16)

        @pl.loop(0, groups)
        def _(k):
            a_copy(k).wait()
            t0 = x_ref[pl.ds(k * 8, 4)].reshape(BLK, 128)
            t1 = x_ref[pl.ds(k * 8 + 4, 4)].reshape(BLK, 128)
            left_half = jnp.concatenate(
                [jnp.where(low, t0, zero), jnp.where(low, zero, t0), zero, zero], axis=0
            )
            right_half = jnp.concatenate(
                [zero, zero, jnp.where(low, t1, zero), jnp.where(low, zero, t1)], axis=0
            )
            lhs = jnp.concatenate([left_half, right_half], axis=1)
            rows = pl.ds(k * 4, 4)
            for n in range((SLOTS * BLK + 255) // 256):
                width = min(256, SLOTS * BLK - n * 256)
                rhs = a_buf[rows, :, n * 256 : n * 256 + width].reshape(4 * BLK, width)
                prod = lax.dot_general(
                    lhs, rhs, (((0,), (0,)), ((), ())), preferred_element_type=jnp.float32
                ).astype(jnp.bfloat16)
                l_buf[rows, 2 * n] = prod[:, :128].reshape(4, BLK, 128)
                l_buf[rows, 2 * n + 1, :, : width - 128] = prod[:, 128:].reshape(4, BLK, width - 128)
            l_copy(k).start()

    order = sorted((ORDER[name] + part * pace, name, part) for name in stages for part in range(chunks))
    for _, name, part in order:
        step(name, part)

    for yy in range(Y):
        for zz in range(2):
            for part in range(chunks):
                arrived(partner, yy, zz, part)
    mine.wait()

    for part in range(chunks):
        for to, index in ((me_other, 0), (me_yf, 2), (me_yb, 3), (me_part, 4)):
            own_copy(to, index, part).wait_send()

        @pl.when(has_far)
        def _(part=part):
            own_copy(me_near, 1, part).wait_send()

        for name in stages:
            sent(name, part)

    if with_left:

        @pl.loop(0, groups)
        def _(k):
            l_copy(k).wait()


def gather(piece, matrix_blocks, n_rows, with_left=True, chunks=4, pace=2):
    return pl.pallas_call(
        functools.partial(gather_kernel, n_rows, with_left, chunks, pace),
        out_shape=(
            pltpu.HBM((6 * Y,) + piece.shape, piece.dtype),
            pltpu.HBM((ROWS_DEV, PAIRS, BLK, 128), jnp.bfloat16),
        ),
        in_specs=[pl.BlockSpec(memory_space=pltpu.VMEM), pl.BlockSpec(memory_space=pltpu.HBM)],
        out_specs=(pl.BlockSpec(memory_space=pltpu.HBM), pl.BlockSpec(memory_space=pltpu.HBM)),
        scratch_shapes=[
            pltpu.VMEM((ROWS_DEV, BLK, SLOTS * BLK), jnp.bfloat16),
            pltpu.VMEM((ROWS_DEV, PAIRS, BLK, 128), jnp.bfloat16),
            pltpu.SemaphoreType.DMA((23, chunks)),
            pltpu.SemaphoreType.DMA((6 * Y, chunks)),
            pltpu.SemaphoreType.DMA,
            pltpu.SemaphoreType.DMA((ROWS_DEV // 4,)),
            pltpu.SemaphoreType.DMA((ROWS_DEV // 4,)),
        ],
        compiler_params=pltpu.CompilerParams(
            collective_id=0, has_side_effects=True, vmem_limit_bytes=32 << 20
        ),
        name="gather_left",
    )(piece, pltpu.with_memory_space_constraint(matrix_blocks, pltpu.HBM))


def entry_kernel(unroll, n_rows, own_ref, count_ref, slab_ref, col_ref, g_hbm, l_hbm, out_ref, g_ref, agg_ref, l_ref, acc, tab, words, g_sem, agg_sem, l_sem, tab_sem):
    n_dev = 6 * Y
    trash = 2 * AGG_DEV * n_dev
    half = lax.broadcasted_iota(jnp.int32, (BLK, 128), 1) // BLK
    slab = slab_ref[0]
    first = jnp.where(slab > 0, 0, ROWS_DEV * 2 * Y)
    last = jnp.where(slab < n_rows - 1, ROWS_DEV * 6 * Y, ROWS_DEV * 4 * Y)
    groups = ROWS_DEV * PAIRS // 64

    def agg_copy(k):
        return pltpu.make_async_copy(g_hbm.at[k, PIECE - 1], agg_ref.at[k], agg_sem.at[k])

    def g_copy(k):
        return pltpu.make_async_copy(
            g_hbm.at[k, pl.ds(0, PIECE - 1)], g_ref.at[pl.ds(k * (PIECE - 1), PIECE - 1)], g_sem.at[k]
        )

    def l_copy(k):
        span = pl.ds(k * 64, 64)
        return pltpu.make_async_copy(l_hbm.at[span], l_ref.at[span], l_sem.at[k])

    @pl.loop(0, n_dev)
    def _(k):
        agg_copy(k).start()

    @pl.loop(0, n_dev)
    def _(k):
        g_copy(k).start()

    @pl.loop(0, groups)
    def _(k):
        l_copy(k).start()

    lane = lax.broadcasted_iota(jnp.int32, (1, 128), 1)
    spot = lax.broadcasted_iota(jnp.int32, (8, 128), 0) * 128 + lax.broadcasted_iota(jnp.int32, (8, 128), 1)
    cols = jnp.zeros((8, 128), jnp.int32)
    meta = jnp.zeros((8, 128), jnp.int32)
    total = 0
    for i in range(ROWS_DEV):
        begin = total
        total = total + count_ref[i]
        row = jnp.concatenate([col_ref[pl.ds(i, 1), :], jnp.zeros((1, 128 - SLOTS), jnp.int32)], axis=1)
        row = jnp.broadcast_to(pltpu.roll(row, begin & 127, 1), (8, 128))
        here = (spot >= begin) & (spot < total)
        cols = jnp.where(here, row, cols)
        meta = jnp.where(here, (begin << 6) + (own_ref[i] << 5) + i, meta)
    used = spot < total
    slots = spot - (meta >> 6)
    side = cols & 1

    @pl.loop(0, n_dev)
    def _(k):
        agg_copy(k).wait()

    aggs = jnp.zeros((8, 128), jnp.int32)
    for k in range(n_dev // 4):
        row = jnp.zeros((1, 128), jnp.int32)
        for q in range(4):
            tile = agg_ref[4 * k + q].astype(jnp.float32)[:1].astype(jnp.int32)
            row = row + jnp.where(lane // 32 == q, tile & 1, 0)
        row = jnp.broadcast_to(row, (8, 128))
        got = jnp.take_along_axis(row, cols & 127, axis=1, mode="promise_in_bounds")
        aggs = jnp.where(cols >> 7 == k, got, aggs)
    seg = ((meta >> 5) & 1) * (2 * n_dev) + (cols >> 5) * 2 + (aggs ^ side)
    tab[pl.ds(0, 8), :] = jnp.where(used & (cols >= first) & (cols < last), seg, trash)
    tab[pl.ds(8, 8), :] = cols >> 1
    tab[pl.ds(16, 8), :] = jnp.where(used, (meta & 31) * PAIRS + (slots >> 1), ROWS_DEV * PAIRS - 1)
    tab[pl.ds(24, 8), :] = (slots & 1) * BLK
    tab[pl.ds(32, 8), :] = side
    to_words = pltpu.make_async_copy(tab, words, tab_sem)
    to_words.start()

    @pl.loop(0, trash)
    def _(k):
        acc[k] = jnp.zeros((BLK, 128), jnp.float32)

    to_words.wait()

    @pl.loop(0, n_dev)
    def _(k):
        g_copy(k).wait()

    def body(c, ready):
        base = c * unroll
        r0 = base >> 7
        c0 = base & 127
        need = (words[16 + r0, c0 + unroll - 1] >> 6) + 1

        @pl.loop(ready, need)
        def _(k):
            l_copy(k).wait()

        prods = []
        for u in range(unroll):
            right = g_ref[pl.ds(words[8 + r0, c0 + u] * 4, 4)].reshape(BLK, 128)
            left = pltpu.roll(l_ref[words[16 + r0, c0 + u]], words[24 + r0, c0 + u], 1)[:, :BLK]
            prods.append(jnp.dot(left, right, preferred_element_type=jnp.float32))
        for u, prod in enumerate(prods):
            acc[words[r0, c0 + u]] += jnp.where(half == words[32 + r0, c0 + u], prod, 0.0)
        return jnp.maximum(ready, need)

    ready = lax.fori_loop(0, (total + unroll - 1) // unroll, body, 0)

    @pl.loop(ready, groups)
    def _(k):
        l_copy(k).wait()

    for a in range(AGG_DEV):

        @pl.loop(0, n_dev, unroll=6)
        def _(w):
            s = (a * n_dev + w) * 2
            pair = acc[s] + pltpu.roll(acc[s + 1], BLK, 1)
            out_ref[a, :, pl.ds(pl.multiple_of(w * 128, 128), 128)] = pair


def entries(cols, counts, own, slab, gathered, left, n_rows, chunk=64):
    n_dev = 6 * Y
    return pl.pallas_call(
        functools.partial(entry_kernel, chunk, n_rows),
        out_shape=jax.ShapeDtypeStruct((AGG_DEV, BLK, n_dev * AGG_DEV * BLK), jnp.float32),
        in_specs=[pl.BlockSpec(memory_space=pltpu.SMEM)] * 3
        + [pl.BlockSpec(memory_space=pltpu.VMEM)]
        + [pl.BlockSpec(memory_space=pltpu.HBM)] * 2,
        out_specs=pl.BlockSpec(memory_space=pltpu.VMEM),
        scratch_shapes=[
            pltpu.VMEM((n_dev * (PIECE - 1), 16, 128), jnp.bfloat16),
            pltpu.VMEM((n_dev, 16, 128), jnp.bfloat16),
            pltpu.VMEM((ROWS_DEV * PAIRS, BLK, 128), jnp.bfloat16),
            pltpu.VMEM((2 * AGG_DEV * n_dev + 1, BLK, 128), jnp.float32),
            pltpu.VMEM((40, 128), jnp.int32),
            pltpu.SMEM((40, 128), jnp.int32),
            pltpu.SemaphoreType.DMA((n_dev,)),
            pltpu.SemaphoreType.DMA((n_dev,)),
            pltpu.SemaphoreType.DMA((ROWS_DEV * PAIRS // 64,)),
            pltpu.SemaphoreType.DMA,
        ],
        compiler_params=pltpu.CompilerParams(vmem_limit_bytes=44 << 20),
        name="entries",
    )(
        own,
        counts,
        slab,
        cols,
        pltpu.with_memory_space_constraint(gathered, pltpu.HBM),
        pltpu.with_memory_space_constraint(left.reshape(ROWS_DEV * PAIRS, BLK, 128), pltpu.HBM),
    )


def per_device(matrix_blocks, restrict, columns, counts, aggregate):
    n_rows = lax.axis_size("rows")
    slab = lax.axis_index("rows").astype(jnp.int32).reshape(1)
    tiles = restrict.reshape(TILES, 2, BLK, BLK).transpose(0, 3, 1, 2).reshape(TILES * 4, 16, 128)
    agg_tile = jnp.broadcast_to(aggregate.astype(jnp.bfloat16)[None, None, None, :], (1, 16, 4, ROWS_DEV))
    agg_tile = agg_tile.reshape(1, 16, 128)
    piece = jnp.concatenate([tiles, agg_tile], axis=0)
    gathered, left = gather(piece, matrix_blocks, n_rows)
    return entries(columns, counts, aggregate, slab, gathered, left, n_rows)


def solution(mesh):
    return jax.shard_map(
        per_device,
        mesh=mesh,
        in_specs=(
            P(("rows", "cols"), None, None),
            P(("rows", "cols"), None),
            P(("rows", "cols"), None),
            P(("rows", "cols")),
            P(("rows", "cols")),
        ),
        out_specs=P(("rows", "cols"), None, None),
        check_vma=False,
    )
```

profile of v0, /device:TPU:7, one launch (start us, length us, event | category | flops | bytes accessed | tf_op | source)
XLA Modules:
  0.0 61.0 jit_solution(13034672440256170466)
XLA Ops:
  0.0 0.0 copy-start.1
  0.0 0.0 copy-start.2
  0.0 0.0 copy-start
  0.0 0.7 %convert_element_type.3 = bf16[32]{0:T(256)(128)(2,1)S(1)} convert(s32[32]{0:T(128)} %own_ref.1) | non-fusion elementwise | flops 32 | bytes 192 | tf_op jit(solution)/shard_map/convert_element_type | solution.py:414
  0.7 0.1 broadcast_in_dim.11
  0.8 1.5 %reshape.18 = bf16[16,2,64,64]{3,2,1,0:T(8,128)(2,1)S(1)} reshape(bf16[32,4096]{1,0:T(8,128)(2,1)} %param.6) | data formatting | bytes 524288 | tf_op jit(solution)/shard_map/reshape | solution.py:413
  2.3 0.4 copy.6
  2.7 0.3 reshape.19
  3.0 45.7 %gather_left.1 = (bf16[24,65,16,128]{3,2,1,0:T(8,128)(2,1)}, bf16[32,14,64,128]{3,2,1,0:T(8,128)(2,1)}) custom-call(bf16[65,16,128]{2,1,0:T(8,128)(2,1)S(1)} %pad_maximum_fusion.x_ref, bf16[32,64,1728]{2,1,0:T(8,128)(2,1)} %a_hbm.1), custom_call_target="tpu_custom_call" | custom-call | tf_op jit(solution)/shard_map/gather_left/pallas_call | solution.py:237
  48.8 0.0 copy-done.1
  48.8 0.0 copy-done.2
  48.8 0.0 copy-done
  48.8 12.2 %entries.1 = f32[2,64,3072]{2,1,0:T(8,128)} custom-call(s32[32]{0:T(128)S(1)} %copy-done.1, s32[32]{0:T(128)S(1)} %copy-done.2, s32[1]{0:T(128)} %bitcast.slab_ref, s32[32,27]{1,0:T(8,128)S(1)} %copy-done, bf16[24,65,16,128]{3,2,1,0:T(8,128)(2,1)} %get-tuple-element.7.g_hbm, bf16[448,64,128]{2,1,0:T(8,128)(2,1)} %bitcast.3), custom_call_target="tpu_custom_call" | custom-call | tf_op jit(solution)/shard_map/entries/pallas_call | solution.py:379
  (3 shorter events, 0.0 us)
Async XLA Ops:
  0.0 48.8 %copy-start.1 = (s32[32]{0:T(128)S(1)}, s32[32]{0:T(128)}, u32[]{:S(2)}) copy-start(s32[32]{0:T(128)} %own_ref.1) | copy-start | bytes 388
  0.0 48.8 %copy-start.2 = (s32[32]{0:T(128)S(1)}, s32[32]{0:T(128)}, u32[]{:S(2)}) copy-start(s32[32]{0:T(128)} %count_ref.1) | copy-start | bytes 388
  0.0 48.8 %copy-start = (s32[32,27]{1,0:T(8,128)S(1)}, s32[32,27]{1,0:T(8,128)}, u32[]{:S(2)}) copy-start(s32[32,27]{1,0:T(8,128)} %col_ref.1) | copy-start | bytes 10372
where the time goes:
time: 61.6 us; the launch traced here: 61 us
  Pallas kernels  57.9 us (94%)
  local copies, waits for them, and re-layouts  2.25 us (4%)
  other arithmetic  0.75 us (1%)
    pallas_call x1, Pallas kernels, gather(): pl.pallas_call(functools.partial(gather_kernel, n_rows, with_left, chunks...  45.7 us
    pallas_call x1, Pallas kernels, entries(): pl.pallas_call(functools.partial(entry_kernel, chunk, n_rows), out_shape=...  12.2 us
    reshape x3, local copies, waits for them, and re-layouts, per_device(): restrict.reshape(TILES, 2, BLK, BLK).transpose(0, 3, 1, 2)  2.14 us

commit v1 on v0

--- a/solution.py
+++ b/solution.py
@@ -18,8 +18,8 @@
 PAIRS = (SLOTS + 1) // 2
 MESH = pl.DeviceIdType.MESH
 ORDER = {
-    "own_b": 4, "own_f": 5, "near_0": 8, "other_0": 10, "own_2": 12, "other_f": 17, "near_b": 17.5, "other_b": 18,
-    "other_2": 22, "back_0": 24, "back_f": 27, "near_f": 27.5, "back_b": 28, "near_2": 28.5, "back_2": 31,
+    "own_b": 1.7, "own_f": 5, "other_0": 7.4, "near_0": 9, "own_2": 12, "other_f": 12.3, "other_b": 18, "near_b": 21.2,
+    "back_b": 21.4, "other_2": 22, "back_0": 24, "near_2": 28.5, "back_f": 29.3, "back_2": 34.1, "near_f": 34.4,
 }
 
 
@@ -114,13 +114,17 @@
         "back_2": (own_other, y2, True, [(me_part, 22)]),
     }
 
+    def passed_on(name, part, do):
+        (slab, zz), yy, needs_far, targets = stages[name]
+        for to, index in targets:
+            do(relay(slab, yy, zz, to, index, part))
+
     def step(name, part):
-        (slab, zz), yy, needs_far, targets = stages[name]
+        (slab, zz), yy, needs_far, _ = stages[name]
 
         def run():
             arrived(slab, yy, zz, part)
-            for to, index in targets:
-                relay(slab, yy, zz, to, index, part).start()
+            passed_on(name, part, lambda c: c.start())
 
         if needs_far:
             pl.when(has_far)(run)
@@ -128,13 +132,10 @@
             run()
 
     def sent(name, part):
-        (slab, zz), yy, needs_far, targets = stages[name]
-
         def run():
-            for to, index in targets:
-                relay(slab, yy, zz, to, index, part).wait_send()
-
-        if needs_far:
+            passed_on(name, part, lambda c: c.wait_send())
+
+        if stages[name][2]:
             pl.when(has_far)(run)
         else:
             run()
@@ -374,7 +375,7 @@
             out_ref[a, :, pl.ds(pl.multiple_of(w * 128, 128), 128)] = pair
 
 
-def entries(cols, counts, own, slab, gathered, left, n_rows, chunk=64):
+def entries(cols, counts, own, slab, gathered, left, n_rows, chunk=128):
     n_dev = 6 * Y
     return pl.pallas_call(
         functools.partial(entry_kernel, chunk, n_rows),

time: 61.6 us -> 59.1 us (0.959)
  the two profiles are of different devices: /device:TPU:7 before, /device:TPU:10 now
where the time goes in v1:
time: 59.1 us; the launch traced here: 59 us
  Pallas kernels  55.9 us (95%)
  local copies, waits for them, and re-layouts  2.25 us (4%)
  other arithmetic  0.75 us (1%)
    pallas_call x1, Pallas kernels, gather(): pl.pallas_call(functools.partial(gather_kernel, n_rows, with_left, chunks...  41.9 us
    pallas_call x1, Pallas kernels, entries(): pl.pallas_call(functools.partial(entry_kernel, chunk, n_rows), out_shape=...  13.9 us
    reshape x3, local copies, waits for them, and re-layouts, per_device(): restrict.reshape(TILES, 2, BLK, BLK).transpose(0, 3, 1, 2)  2.14 us

profile of v1, /device:TPU:10, one launch (start us, length us, event | category | flops | bytes accessed | tf_op | source)
XLA Modules:
  0.0 59.0 jit_solution(2530730479091559737)
XLA Ops:
  0.0 0.0 copy-start.1
  0.0 0.0 copy-start.2
  0.0 0.0 copy-start
  0.0 0.7 %convert_element_type.3 = bf16[32]{0:T(256)(128)(2,1)S(1)} convert(s32[32]{0:T(128)} %own_ref.1) | non-fusion elementwise | flops 32 | bytes 192 | tf_op jit(solution)/shard_map/convert_element_type | solution.py:415
  0.7 0.1 broadcast_in_dim.11
  0.8 1.5 %reshape.18 = bf16[16,2,64,64]{3,2,1,0:T(8,128)(2,1)S(1)} reshape(bf16[32,4096]{1,0:T(8,128)(2,1)} %param.6) | data formatting | bytes 524288 | tf_op jit(solution)/shard_map/reshape | solution.py:414
  2.3 0.4 copy.6
  2.7 0.3 reshape.19
  3.0 41.9 %gather_left.1 = (bf16[24,65,16,128]{3,2,1,0:T(8,128)(2,1)}, bf16[32,14,64,128]{3,2,1,0:T(8,128)(2,1)}) custom-call(bf16[65,16,128]{2,1,0:T(8,128)(2,1)S(1)} %pad_maximum_fusion.x_ref, bf16[32,64,1728]{2,1,0:T(8,128)(2,1)} %a_hbm.1), custom_call_target="tpu_custom_call" | custom-call | tf_op jit(solution)/shard_map/gather_left/pallas_call | solution.py:238
  45.0 0.0 copy-done.1
  45.0 0.0 copy-done.2
  45.0 0.0 copy-done
  45.0 13.9 %entries.1 = f32[2,64,3072]{2,1,0:T(8,128)} custom-call(s32[32]{0:T(128)S(1)} %copy-done.1, s32[32]{0:T(128)S(1)} %copy-done.2, s32[1]{0:T(128)} %bitcast.slab_ref, s32[32,27]{1,0:T(8,128)S(1)} %copy-done, bf16[24,65,16,128]{3,2,1,0:T(8,128)(2,1)} %get-tuple-element.7.g_hbm, bf16[448,64,128]{2,1,0:T(8,128)(2,1)} %bitcast.3), custom_call_target="tpu_custom_call" | custom-call | tf_op jit(solution)/shard_map/entries/pallas_call | solution.py:380
  (3 shorter events, 0.0 us)
Async XLA Ops:
  0.0 45.0 %copy-start.1 = (s32[32]{0:T(128)S(1)}, s32[32]{0:T(128)}, u32[]{:S(2)}) copy-start(s32[32]{0:T(128)} %own_ref.1) | copy-start | bytes 388
  0.0 45.0 %copy-start.2 = (s32[32]{0:T(128)S(1)}, s32[32]{0:T(128)}, u32[]{:S(2)}) copy-start(s32[32]{0:T(128)} %count_ref.1) | copy-start | bytes 388
  0.0 45.0 %copy-start = (s32[32,27]{1,0:T(8,128)S(1)}, s32[32,27]{1,0:T(8,128)}, u32[]{:S(2)}) copy-start(s32[32,27]{1,0:T(8,128)} %col_ref.1) | copy-start | bytes 10372

commit v2 on v1

--- a/solution.py
+++ b/solution.py
@@ -18,8 +18,8 @@
 PAIRS = (SLOTS + 1) // 2
 MESH = pl.DeviceIdType.MESH
 ORDER = {
-    "own_b": 1.7, "own_f": 5, "other_0": 7.4, "near_0": 9, "own_2": 12, "other_f": 12.3, "other_b": 18, "near_b": 21.2,
-    "back_b": 21.4, "other_2": 22, "back_0": 24, "near_2": 28.5, "back_f": 29.3, "back_2": 34.1, "near_f": 34.4,
+    "own_b": 1, "own_f": 6.5, "other_0": 7.4, "own_2": 12, "other_f": 12.3, "near_0": 14.4, "other_b": 18, "near_b": 21.2,
+    "back_b": 21.4, "other_2": 22, "back_0": 25.6, "near_2": 28.5, "back_f": 29.3, "back_2": 34.1, "near_f": 34.4,
 }
 
 
@@ -167,11 +167,12 @@
     pl.semaphore_wait(barrier, 4 + has_far.astype(jnp.int32))
 
     for part in range(chunks):
+        own_copy(me_other, 0, part).start()
+
         @pl.when(has_far)
         def _(part=part):
             own_copy(me_near, 1, part).start()
 
-        own_copy(me_other, 0, part).start()
         own_copy(me_yf, 2, part).start()
         own_copy(me_yb, 3, part).start()
         own_copy(me_part, 4, part).start()
@@ -411,7 +412,7 @@
 def per_device(matrix_blocks, restrict, columns, counts, aggregate):
     n_rows = lax.axis_size("rows")
     slab = lax.axis_index("rows").astype(jnp.int32).reshape(1)
-    tiles = restrict.reshape(TILES, 2, BLK, BLK).transpose(0, 3, 1, 2).reshape(TILES * 4, 16, 128)
+    tiles = jnp.swapaxes(restrict.reshape(TILES, 2 * BLK, BLK), 1, 2).reshape(TILES * 4, 16, 128)
     agg_tile = jnp.broadcast_to(aggregate.astype(jnp.bfloat16)[None, None, None, :], (1, 16, 4, ROWS_DEV))
     agg_tile = agg_tile.reshape(1, 16, 128)
     piece = jnp.concatenate([tiles, agg_tile], axis=0)

time: 59.1 us -> 58.5 us (0.990)
  the two profiles are of different devices: /device:TPU:10 before, /device:TPU:39 now
where the time goes in v2:
time: 58.5 us; the launch traced here: 58.1 us
  Pallas kernels  55.4 us (95%)
  local copies, waits for them, and re-layouts  1.81 us (3%)
  other arithmetic  0.75 us (1%)
    pallas_call x1, Pallas kernels, gather(): pl.pallas_call(functools.partial(gather_kernel, n_rows, with_left, chunks...  41.5 us
    pallas_call x1, Pallas kernels, entries(): pl.pallas_call(functools.partial(entry_kernel, chunk, n_rows), out_shape=...  13.9 us
    reshape x1, local copies, waits for them, and re-layouts, per_device(): restrict.reshape(TILES, 2 * BLK, BLK)  1.47 us

profile of v2, /device:TPU:39, one launch (start us, length us, event | category | flops | bytes accessed | tf_op | source)
XLA Modules:
  0.0 58.1 jit_solution(14605130688464164172)
XLA Ops:
  0.0 0.0 copy-start.1
  0.0 0.0 copy-start.2
  0.0 0.0 copy-start
  0.0 0.7 %convert_element_type.3 = bf16[32]{0:T(256)(128)(2,1)S(1)} convert(s32[32]{0:T(128)} %own_ref.1) | non-fusion elementwise | flops 32 | bytes 192 | tf_op jit(solution)/shard_map/convert_element_type | solution.py:416
  0.7 0.1 broadcast_in_dim.11
  0.8 1.5 %reshape.18 = bf16[16,128,64]{2,1,0:T(8,128)(2,1)S(1)} reshape(bf16[32,4096]{1,0:T(8,128)(2,1)} %param.6) | data formatting | bytes 524288 | tf_op jit(solution)/shard_map/reshape | solution.py:415
  2.3 0.2 copy.7
  2.6 41.5 %gather_left.1 = (bf16[24,65,16,128]{3,2,1,0:T(8,128)(2,1)}, bf16[32,14,64,128]{3,2,1,0:T(8,128)(2,1)}) custom-call(bf16[65,16,128]{2,1,0:T(8,128)(2,1)S(1)} %pad_maximum_fusion.x_ref, bf16[32,64,1728]{2,1,0:T(8,128)(2,1)} %a_hbm.1), custom_call_target="tpu_custom_call" | custom-call | tf_op jit(solution)/shard_map/gather_left/pallas_call | solution.py:239
  44.1 0.0 copy-done.1
  44.1 0.0 copy-done.2
  44.1 0.0 copy-done
  44.1 13.9 %entries.1 = f32[2,64,3072]{2,1,0:T(8,128)} custom-call(s32[32]{0:T(128)S(1)} %copy-done.1, s32[32]{0:T(128)S(1)} %copy-done.2, s32[1]{0:T(128)} %bitcast.slab_ref, s32[32,27]{1,0:T(8,128)S(1)} %copy-done, bf16[24,65,16,128]{3,2,1,0:T(8,128)(2,1)} %get-tuple-element.7.g_hbm, bf16[448,64,128]{2,1,0:T(8,128)(2,1)} %bitcast.4), custom_call_target="tpu_custom_call" | custom-call | tf_op jit(solution)/shard_map/entries/pallas_call | solution.py:381
  (3 shorter events, 0.0 us)
Async XLA Ops:
  0.0 44.1 %copy-start.1 = (s32[32]{0:T(128)S(1)}, s32[32]{0:T(128)}, u32[]{:S(2)}) copy-start(s32[32]{0:T(128)} %own_ref.1) | copy-start | bytes 388
  0.0 44.1 %copy-start.2 = (s32[32]{0:T(128)S(1)}, s32[32]{0:T(128)}, u32[]{:S(2)}) copy-start(s32[32]{0:T(128)} %count_ref.1) | copy-start | bytes 388
  0.0 44.1 %copy-start = (s32[32,27]{1,0:T(8,128)S(1)}, s32[32,27]{1,0:T(8,128)}, u32[]{:S(2)}) copy-start(s32[32,27]{1,0:T(8,128)} %col_ref.1) | copy-start | bytes 10372

commit v3 on v2

--- a/solution.py
+++ b/solution.py
@@ -260,7 +260,7 @@
     )(piece, pltpu.with_memory_space_constraint(matrix_blocks, pltpu.HBM))
 
 
-def entry_kernel(unroll, n_rows, own_ref, count_ref, slab_ref, col_ref, g_hbm, l_hbm, out_ref, g_ref, agg_ref, l_ref, acc, tab, words, g_sem, agg_sem, l_sem, tab_sem):
+def entry_kernel(unroll, n_rows, own_ref, count_ref, slab_ref, col_ref, g_hbm, l_hbm, out_hbm, out_ref, out_sem, g_ref, agg_ref, l_ref, acc, tab, words, g_sem, agg_sem, l_sem, tab_sem):
     n_dev = 6 * Y
     trash = 2 * AGG_DEV * n_dev
     half = lax.broadcasted_iota(jnp.int32, (BLK, 128), 1) // BLK
@@ -355,7 +355,9 @@
         prods = []
         for u in range(unroll):
             right = g_ref[pl.ds(words[8 + r0, c0 + u] * 4, 4)].reshape(BLK, 128)
-            left = pltpu.roll(l_ref[words[16 + r0, c0 + u]], words[24 + r0, c0 + u], 1)[:, :BLK]
+            left = l_ref[words[16 + r0, c0 + u]]
+            left = jnp.where(half * BLK == words[24 + r0, c0 + u], left, jnp.bfloat16(0))
+            right = jnp.concatenate([right, right], axis=0)
             prods.append(jnp.dot(left, right, preferred_element_type=jnp.float32))
         for u, prod in enumerate(prods):
             acc[words[r0, c0 + u]] += jnp.where(half == words[32 + r0, c0 + u], prod, 0.0)
@@ -375,17 +377,24 @@
             pair = acc[s] + pltpu.roll(acc[s + 1], BLK, 1)
             out_ref[a, :, pl.ds(pl.multiple_of(w * 128, 128), 128)] = pair
 
+        pltpu.make_async_copy(out_ref.at[a], out_hbm.at[a], out_sem.at[a]).start()
+
+    for a in range(AGG_DEV):
+        pltpu.make_async_copy(out_ref.at[a], out_hbm.at[a], out_sem.at[a]).wait()
+
 
 def entries(cols, counts, own, slab, gathered, left, n_rows, chunk=128):
     n_dev = 6 * Y
     return pl.pallas_call(
         functools.partial(entry_kernel, chunk, n_rows),
-        out_shape=jax.ShapeDtypeStruct((AGG_DEV, BLK, n_dev * AGG_DEV * BLK), jnp.float32),
+        out_shape=pltpu.HBM((AGG_DEV, BLK, n_dev * AGG_DEV * BLK), jnp.float32),
         in_specs=[pl.BlockSpec(memory_space=pltpu.SMEM)] * 3
         + [pl.BlockSpec(memory_space=pltpu.VMEM)]
         + [pl.BlockSpec(memory_space=pltpu.HBM)] * 2,
-        out_specs=pl.BlockSpec(memory_space=pltpu.VMEM),
+        out_specs=pl.BlockSpec(memory_space=pltpu.HBM),
         scratch_shapes=[
+            pltpu.VMEM((AGG_DEV, BLK, n_dev * AGG_DEV * BLK), jnp.float32),
+            pltpu.SemaphoreType.DMA((AGG_DEV,)),
             pltpu.VMEM((n_dev * (PIECE - 1), 16, 128), jnp.bfloat16),
             pltpu.VMEM((n_dev, 16, 128), jnp.bfloat16),
             pltpu.VMEM((ROWS_DEV * PAIRS, BLK, 128), jnp.bfloat16),

time: 58.5 us -> 57.4 us (0.981)
  the two profiles are of different devices: /device:TPU:39 before, /device:TPU:31 now
where the time goes in v3:
time: 57.4 us; the launch traced here: 57.3 us
  Pallas kernels  54.7 us (95%)
  local copies, waits for them, and re-layouts  1.81 us (3%)
  other arithmetic  0.75 us (1%)
    pallas_call x1, Pallas kernels, gather(): pl.pallas_call(functools.partial(gather_kernel, n_rows, with_left, chunks...  41.5 us
    pallas_call x1, Pallas kernels, entries(): pl.pallas_call(functools.partial(entry_kernel, chunk, n_rows), out_shape=...  13.1 us
    reshape x1, local copies, waits for them, and re-layouts, per_device(): restrict.reshape(TILES, 2 * BLK, BLK)  1.47 us

profile of v3, /device:TPU:31, one launch (start us, length us, event | category | flops | bytes accessed | tf_op | source)
XLA Modules:
  0.0 57.3 jit_solution(11509336291730746993)
XLA Ops:
  0.0 0.0 copy-start.1
  0.0 0.0 copy-start.2
  0.0 0.0 copy-start
  0.0 0.7 %convert_element_type.3 = bf16[32]{0:T(256)(128)(2,1)S(1)} convert(s32[32]{0:T(128)} %own_ref.1) | non-fusion elementwise | flops 32 | bytes 192 | tf_op jit(solution)/shard_map/convert_element_type | solution.py:425
  0.7 0.1 broadcast_in_dim.11
  0.8 1.5 %reshape.18 = bf16[16,128,64]{2,1,0:T(8,128)(2,1)S(1)} reshape(bf16[32,4096]{1,0:T(8,128)(2,1)} %param.6) | data formatting | bytes 524288 | tf_op jit(solution)/shard_map/reshape | solution.py:424
  2.3 0.2 copy.7
  2.6 41.5 %gather_left.1 = (bf16[24,65,16,128]{3,2,1,0:T(8,128)(2,1)}, bf16[32,14,64,128]{3,2,1,0:T(8,128)(2,1)}) custom-call(bf16[65,16,128]{2,1,0:T(8,128)(2,1)S(1)} %pad_maximum_fusion.x_ref, bf16[32,64,1728]{2,1,0:T(8,128)(2,1)} %a_hbm.1), custom_call_target="tpu_custom_call" | custom-call | tf_op jit(solution)/shard_map/gather_left/pallas_call | solution.py:239
  44.1 0.0 copy-done.1
  44.1 0.0 copy-done.2
  44.2 0.0 copy-done
  44.2 13.1 %entries.1 = f32[2,64,3072]{2,1,0:T(8,128)} custom-call(s32[32]{0:T(128)S(1)} %copy-done.1, s32[32]{0:T(128)S(1)} %copy-done.2, s32[1]{0:T(128)} %bitcast.slab_ref, s32[32,27]{1,0:T(8,128)S(1)} %copy-done, bf16[24,65,16,128]{3,2,1,0:T(8,128)(2,1)} %get-tuple-element.7.g_hbm, bf16[448,64,128]{2,1,0:T(8,128)(2,1)} %bitcast.4), custom_call_target="tpu_custom_call" | custom-call | tf_op jit(solution)/shard_map/entries/pallas_call | solution.py:388
  (3 shorter events, 0.0 us)
Async XLA Ops:
  0.0 44.1 %copy-start.1 = (s32[32]{0:T(128)S(1)}, s32[32]{0:T(128)}, u32[]{:S(2)}) copy-start(s32[32]{0:T(128)} %own_ref.1) | copy-start | bytes 388
  0.0 44.1 %copy-start.2 = (s32[32]{0:T(128)S(1)}, s32[32]{0:T(128)}, u32[]{:S(2)}) copy-start(s32[32]{0:T(128)} %count_ref.1) | copy-start | bytes 388
  0.0 44.1 %copy-start = (s32[32,27]{1,0:T(8,128)S(1)}, s32[32,27]{1,0:T(8,128)}, u32[]{:S(2)}) copy-start(s32[32,27]{1,0:T(8,128)} %col_ref.1) | copy-start | bytes 10372
